TPU v7x, 32 devices: a whole 2x2x4 slice. The times are simulated.
32 devices in a mesh: dp: 8 (over z, x), space: 4 (over y, core).
Axes of the slice: x: 2, y: 2, z: 4, core: 2. Of those that a mesh axis runs over, the one named last changes fastest.
Arguments:
- images: bfloat16 [256, 24, 24, 384], P('dp', 'space'), may hold values from -6 to 6
- cotangent: bfloat16 [256, 24, 24, 384], P('dp', 'space'), may hold values from -6 to 6
- image_sides: int32 [256], P('dp'), may hold values from 14 to 24, as said below
- keep_flags: int32 [256], P('dp'), may hold values 0 or 1
- depth_kernel: float32 [49, 384], P(None, ('dp', 'space')), may hold values from -0.875 to 0.875
- kernel_moment: float32 [49, 384], P(None, ('dp', 'space')), may hold values from -0.00061035156 to 0.00061035156
- kernel_square: float32 [49, 384], P(None, ('dp', 'space')), may hold values from 4.1600107e-10 to 6.656017e-09
- block_vectors: float32 [5, 384], P(None, ('dp', 'space')), may hold values from -1.5 to 1.5
- vector_moment: float32 [5, 384], P(None, ('dp', 'space')), may hold values from -0.00061035156 to 0.00061035156
- vector_square: float32 [5, 384], P(None, ('dp', 'space')), may hold values from 4.1600107e-10 to 6.656017e-09
- up_weight: float32 [384, 1536], P(None, ('dp', 'space')), may hold values from -0.3125 to 0.3125
- up_moment: float32 [384, 1536], P(None, ('dp', 'space')), may hold values from -0.00061035156 to 0.00061035156
- up_square: float32 [384, 1536], P(None, ('dp', 'space')), may hold values from 4.1600107e-10 to 6.656017e-09
- up_bias: float32 [1536], P(('dp', 'space')), may hold values from -3 to 3
- bias_moment: float32 [1536], P(('dp', 'space')), may hold values from -0.00061035156 to 0.00061035156
- bias_square: float32 [1536], P(('dp', 'space')), may hold values from 4.1600107e-10 to 6.656017e-09
- down_weight: float32 [1536, 384], P(('dp', 'space')), may hold values from -0.15625 to 0.15625
- down_moment: float32 [1536, 384], P(('dp', 'space')), may hold values from -0.00061035156 to 0.00061035156
- down_square: float32 [1536, 384], P(('dp', 'space')), may hold values from 4.1600107e-10 to 6.656017e-09
Outputs:
- out_images: bfloat16 [256, 24, 24, 384], P('dp', 'space')
- grad_images: bfloat16 [256, 24, 24, 384], P('dp', 'space')
- new_kernel: float32 [49, 384], P(None, ('dp', 'space'))
- new_kernel_moment: float32 [49, 384], P(None, ('dp', 'space'))
- new_kernel_square: float32 [49, 384], P(None, ('dp', 'space'))
- new_vectors: float32 [5, 384], P(None, ('dp', 'space'))
- new_vector_moment: float32 [5, 384], P(None, ('dp', 'space'))
- new_vector_square: float32 [5, 384], P(None, ('dp', 'space'))
- new_up: float32 [384, 1536], P(None, ('dp', 'space'))
- new_up_moment: float32 [384, 1536], P(None, ('dp', 'space'))
- new_up_square: float32 [384, 1536], P(None, ('dp', 'space'))
- new_bias: float32 [1536], P(('dp', 'space'))
- new_bias_moment: float32 [1536], P(('dp', 'space'))
- new_bias_square: float32 [1536], P(('dp', 'space'))
- new_down: float32 [1536, 384], P(('dp', 'space'))
- new_down_moment: float32 [1536, 384], P(('dp', 'space'))
- new_down_square: float32 [1536, 384], P(('dp', 'space'))
- grad_norm: float32 [], replicated
Inputs may be any that keep to these rules, and one draw needn't show every extreme that they name: `image_sides`: each image's valid square has one of the sides 24, 18, 14.
All inputs are finite; a program needn't handle non-finite values. No bound on the sum of `keep_flags` on one device may be relied on, other than what follows from the above.
Results may differ from a plain program's by a relative error of at most 0.0055.
Values may be sent and summed in bfloat16 or wider, within the bound.
No kernel may reach another device: no remote copies, remote signals or barrier semaphores. Data moves between devices by JAX's collectives and lax.ppermute only.
A program may use at most 192 MiB of HBM per device.

v0:
```python
import jax
import jax.numpy as jnp
from jax import lax
from jax.sharding import PartitionSpec as P

STEP = 5
keep_scale = 4.0 / 3.0
norm_eps = 1e-06
clip_limit = 1.0
beta_one = 0.9
beta_two = 0.999
adam_eps = 1e-08
decay_rate = 0.05
step_rates = (0.15, 0.5, 0.05, 0.2, 0.025)
inv_root_two = 0.7071067811865476
inv_root_tau = 0.3989422804014327


def conv_rows(padded, kernel, out_rows, out_cols):
    wide = jnp.pad(padded, ((0, 0), (0, 0), (3, 3), (0, 0)))
    running = jnp.zeros((padded.shape[0], out_rows, out_cols, padded.shape[3]), jnp.float32)
    for row_off in range(7):
        for col_off in range(7):
            running = (
                running
                + kernel[row_off * 7 + col_off]
                * wide[:, row_off : row_off + out_rows, col_off : col_off + out_cols, :]
            )
    return running


def kernel_grad(padded, grad_conv):
    wide = jnp.pad(padded, ((0, 0), (0, 0), (3, 3), (0, 0)))
    out_rows = grad_conv.shape[1]
    out_cols = grad_conv.shape[2]
    pieces = [
        jnp.sum(
            wide[:, row_off : row_off + out_rows, col_off : col_off + out_cols, :] * grad_conv,
            axis=(0, 1, 2),
        )
        for row_off in range(7)
        for col_off in range(7)
    ]
    return jnp.stack(pieces)


def adam_update(weight, moment, square, grad_part, factor, step_rate):
    scaled = grad_part * factor
    new_moment = beta_one * moment + (1.0 - beta_one) * scaled
    new_square = beta_two * square + (1.0 - beta_two) * scaled * scaled
    corrected = new_moment / (1.0 - beta_one**STEP)
    spread = jnp.sqrt(new_square / (1.0 - beta_two**STEP))
    new_weight = weight - step_rate * (corrected / (spread + adam_eps) + decay_rate * weight)
    return (new_weight, new_moment, new_square)


def body(
    images,
    cotangent,
    image_sides,
    keep_flags,
    depth_kernel,
    kernel_moment,
    kernel_square,
    block_vectors,
    vector_moment,
    vector_square,
    up_weight,
    up_moment,
    up_square,
    up_bias,
    bias_moment,
    bias_square,
    down_weight,
    down_moment,
    down_square,
):
    up_full, down_full = (
        lax.all_gather(up_weight.astype(jnp.bfloat16), ("dp", "space"), axis=1, tiled=True),
        lax.all_gather(down_weight.astype(jnp.bfloat16), ("dp", "space"), axis=0, tiled=True),
    )
    kernel_full, vector_full, bias_full = (
        lax.all_gather(depth_kernel, ("dp", "space"), axis=1, tiled=True),
        lax.all_gather(block_vectors, ("dp", "space"), axis=1, tiled=True),
        lax.all_gather(up_bias, ("dp", "space"), axis=0, tiled=True),
    )
    map_side = images.shape[2]
    local_images, local_cot = (
        lax.all_to_all(images, "space", split_axis=0, concat_axis=1, tiled=True),
        lax.all_to_all(cotangent, "space", split_axis=0, concat_axis=1, tiled=True),
    )
    img_count = local_images.shape[0]
    first_image = lax.axis_index("space") * img_count
    local_sides = lax.dynamic_slice_in_dim(image_sides, first_image, img_count)
    local_keep = lax.dynamic_slice_in_dim(keep_flags, first_image, img_count)
    row_ids = jnp.arange(map_side, dtype=jnp.int32)
    col_ids = jnp.arange(map_side, dtype=jnp.int32)
    rows_in = row_ids[None, :] < local_sides[:, None]
    cols_in = col_ids[None, :] < local_sides[:, None]
    pixel_mask = (rows_in[:, :, None] & cols_in[:, None, :]).astype(jnp.float32)
    branch_scale = pixel_mask * (local_keep.astype(jnp.float32) * keep_scale)[:, None, None]
    masked = local_images * pixel_mask.astype(jnp.bfloat16)[..., None]
    padded = jnp.pad(masked, ((0, 0), (3, 3), (0, 0), (0, 0)))
    out_rows = local_images.shape[1]
    conv = conv_rows(padded, kernel_full, out_rows, map_side) + vector_full[0]
    chan_mean = jnp.mean(conv, axis=-1, keepdims=True)
    centred = conv - chan_mean
    chan_var = jnp.mean(centred * centred, axis=-1, keepdims=True)
    inv_std = lax.rsqrt(chan_var + norm_eps)
    unit_norm = centred * inv_std
    normed = (unit_norm * vector_full[1] + vector_full[2]).astype(jnp.bfloat16)
    hidden = (
        jnp.einsum("nijc,ch->nijh", normed, up_full, preferred_element_type=jnp.float32) + bias_full
    )
    normal_cdf = 0.5 * (1.0 + lax.erf(hidden * inv_root_two))
    active = (hidden * normal_cdf).astype(jnp.bfloat16)
    branch = (
        jnp.einsum("nijh,hc->nijc", active, down_full, preferred_element_type=jnp.float32)
        + vector_full[3]
    )
    out_images = (
        local_images.astype(jnp.float32) + branch_scale[..., None] * vector_full[4] * branch
    ).astype(jnp.bfloat16)
    grad_out = local_cot.astype(jnp.float32)
    grad_branch = (grad_out * branch_scale[..., None] * vector_full[4]).astype(jnp.bfloat16)
    grad_scale = jnp.sum(grad_out * branch_scale[..., None] * branch, axis=(0, 1, 2))
    grad_outbias = jnp.sum(grad_branch.astype(jnp.float32), axis=(0, 1, 2))
    grad_down = jnp.einsum("nijh,nijc->hc", active, grad_branch, preferred_element_type=jnp.float32)
    grad_active = jnp.einsum(
        "nijc,hc->nijh", grad_branch, down_full, preferred_element_type=jnp.float32
    )
    slope = normal_cdf + hidden * inv_root_tau * jnp.exp(-0.5 * hidden * hidden)
    grad_hidden = (grad_active * slope).astype(jnp.bfloat16)
    grad_up = jnp.einsum("nijc,nijh->ch", normed, grad_hidden, preferred_element_type=jnp.float32)
    grad_upbias = jnp.sum(grad_hidden.astype(jnp.float32), axis=(0, 1, 2))
    grad_normed = jnp.einsum(
        "nijh,ch->nijc", grad_hidden, up_full, preferred_element_type=jnp.float32
    )
    grad_gain = jnp.sum(grad_normed * unit_norm, axis=(0, 1, 2))
    grad_shift = jnp.sum(grad_normed, axis=(0, 1, 2))
    scaled_dn = grad_normed * vector_full[1]
    grad_conv = inv_std * (
        scaled_dn
        - jnp.mean(scaled_dn, axis=-1, keepdims=True)
        - unit_norm * jnp.mean(scaled_dn * unit_norm, axis=-1, keepdims=True)
    )
    grad_convbias = jnp.sum(grad_conv, axis=(0, 1, 2))
    grad_rows = jnp.pad(grad_conv, ((0, 0), (3, 3), (0, 0), (0, 0)))
    grad_u = conv_rows(grad_rows, kernel_full[::-1], out_rows, map_side)
    grad_local = (grad_out + pixel_mask[..., None] * grad_u).astype(jnp.bfloat16)
    grad_kernel = kernel_grad(padded, grad_conv)
    grad_vectors = jnp.stack([grad_convbias, grad_gain, grad_shift, grad_outbias, grad_scale])
    out_tiles, grad_tiles = (
        lax.all_to_all(out_images, "space", split_axis=1, concat_axis=0, tiled=True),
        lax.all_to_all(grad_local, "space", split_axis=1, concat_axis=0, tiled=True),
    )
    local_grads = (grad_kernel, grad_vectors, grad_up, grad_upbias, grad_down)
    summed = lax.psum(
        (local_grads[0], local_grads[1], local_grads[2], local_grads[3], local_grads[4]),
        ("dp", "space"),
    )
    total_squares = sum((jnp.sum(g * g) for g in summed))
    owner = lax.axis_index(("dp", "space"))
    shard_grads = (
        lax.dynamic_slice_in_dim(
            summed[0], owner * depth_kernel.shape[1], depth_kernel.shape[1], 1
        ),
        lax.dynamic_slice_in_dim(
            summed[1], owner * block_vectors.shape[1], block_vectors.shape[1], 1
        ),
        lax.dynamic_slice_in_dim(summed[2], owner * up_weight.shape[1], up_weight.shape[1], 1),
        lax.dynamic_slice_in_dim(summed[3], owner * up_bias.shape[0], up_bias.shape[0], 0),
        lax.dynamic_slice_in_dim(summed[4], owner * down_weight.shape[0], down_weight.shape[0], 0),
    )
    grad_norm = jnp.sqrt(total_squares)
    factor = clip_limit / jnp.maximum(grad_norm, clip_limit)
    states = (
        (depth_kernel, kernel_moment, kernel_square),
        (block_vectors, vector_moment, vector_square),
        (up_weight, up_moment, up_square),
        (up_bias, bias_moment, bias_square),
        (down_weight, down_moment, down_square),
    )
    results = []
    for (weight, moment, square), grad_part, step_rate in zip(states, shard_grads, step_rates):
        results.extend(adam_update(weight, moment, square, grad_part, factor, step_rate))
    return (
        out_tiles,
        grad_tiles,
        results[0],
        results[1],
        results[2],
        results[3],
        results[4],
        results[5],
        results[6],
        results[7],
        results[8],
        results[9],
        results[10],
        results[11],
        results[12],
        results[13],
        results[14],
        grad_norm,
    )


def solution(mesh):
    in_specs = (
        P("dp", "space", None, None),
        P("dp", "space", None, None),
        P("dp"),
        P("dp"),
        P(None, ("dp", "space")),
        P(None, ("dp", "space")),
        P(None, ("dp", "space")),
        P(None, ("dp", "space")),
        P(None, ("dp", "space")),
        P(None, ("dp", "space")),
        P(None, ("dp", "space")),
        P(None, ("dp", "space")),
        P(None, ("dp", "space")),
        P(("dp", "space")),
        P(("dp", "space")),
        P(("dp", "space")),
        P(("dp", "space"), None),
        P(("dp", "space"), None),
        P(("dp", "space"), None),
    )
    out_specs = (
        P("dp", "space", None, None),
        P("dp", "space", None, None),
        P(None, ("dp", "space")),
        P(None, ("dp", "space")),
        P(None, ("dp", "space")),
        P(None, ("dp", "space")),
        P(None, ("dp", "space")),
        P(None, ("dp", "space")),
        P(None, ("dp", "space")),
        P(None, ("dp", "space")),
        P(None, ("dp", "space")),
        P(("dp", "space")),
        P(("dp", "space")),
        P(("dp", "space")),
        P(("dp", "space"), None),
        P(("dp", "space"), None),
        P(("dp", "space"), None),
        P(),
    )
    return jax.shard_map(body, mesh=mesh, in_specs=in_specs, out_specs=out_specs, check_vma=False)
```

profile of v0, /device:TPU:12, one launch (start us, length us, event | category | flops | bytes accessed | tf_op | source)
XLA Modules:
  0.0 850.3 jit_solution(6092713917045323219)
XLA Ops:
  7.2 4.4 all-to-all-start
  13.1 38.7 %all-to-all-done = bf16[32,6,24,384]{3,2,1,0:T(8,128)(2,1)S(1)} async-done(((bf16[32,6,24,384]{3,2,1,0:T(8,128)(2,1)}), bf16[32,6,24,384]{3,2,1,0:T(8,128)(2,1)S(1)}, u32[]{:S(2)}, u32[]{:S(2)}) %all-to-all-start) | async-done | bytes 3538976 | tf_op jit(solution)/shard_map/all_to_all | solution.py:89
  51.9 6.4 all-to-all-start.2
  59.8 64.6 %all-gather = f32[32,12,5]{1,2,0:T(8,128)S(1)} all-gather(f32[1,12,5]{1,2,0:T(8,128)S(1)} %bitcast.83), channel_id=1, replica_groups=mesh['dp'=8,'space'=4] {'dp','space'}, dimensions={0}, use_global_device_ids=true | all-gather | bytes 7920 | tf_op jit(solution)/shard_map/all_gather | solution.py:84
  126.6 43.0 %all-gather.1 = f32[32,12,49]{2,1,0:T(8,128)} all-gather(f32[1,12,49]{2,1,0:T(8,128)S(1)} %bitcast.81), channel_id=1, replica_groups=mesh['dp'=8,'space'=4] {'dp','space'}, dimensions={0}, use_global_device_ids=true | all-gather | bytes 77616 | tf_op jit(solution)/shard_map/all_gather | solution.py:83
  171.6 45.5 %all-reduce.4 = f32[1536]{0:T(1024)} all-reduce(f32[1536]{0:T(1024)S(1)} %dynamic-update-slice), channel_id=1, replica_groups=mesh['dp'=8,'space'=4] {'dp','space'}, use_global_device_ids=true, to_apply=%add.4 | all-reduce | flops 1536 | bytes 12288
  221.4 2.6 slice_reduce_fusion.47
  224.0 2.6 slice_reduce_fusion.48
  229.4 5.5 copy.165
  238.3 59.4 %fusion.231 = (f32[8,24,24]{2,1,0:T(8,128)S(1)}, f32[8,24,24,384]{3,2,1,0:T(8,128)S(1)}) fusion(f32[384]{0:T(512)} %get-tuple-element.179, f32[384]{0:T(512)S(1)} %copy-done.48, f32[384]{0:T(512)S(1)} %copy-done.49, f32[384]{0:T(512)S(1)} %copy-done.50, bf16[8,30,24,384]{3,2,1,0:T(8,128)(2,1)S(1)} %pad.17, f32[384]{0:T(512)S(1)} %copy-done.51, ...), kind=kLoop, calls=%fused_computation.507 | loop fusion | flops 267185664 | bytes 36440576 | tf_op jit(solution)/shard_map/reduce_sum | solution.py:106
  297.8 2.8 copy-done.1
  302.8 18.7 %multiply_convert_fusion = (bf16[8,24,24,1536]{3,2,1,0:T(8,128)(2,1)}, f32[8,24,24,1536]{3,2,1,0:T(8,128)}) fusion(f32[1536]{0:T(1024)S(1)} %copy-done.85, bf16[384,1536]{0,1:T(8,128)(2,1)} %all-gather.5.cloned.1.call-done, f32[8,24,24,384]{3,2,1,0:T(8,128)} %copy-done.1, f32[384]{0:T(512)} %get-tuple-element.177, f32[384]{0:T(512)S(1)} %copy-done.64, ...), kind=kOutput, calls=%fused_computation.49 | convolution fusion | flops 5487132672 | bytes 50770944 | tf_op jit(solution)/shard_map/nijc,ch->nijh/dot_general | solution.py:113
  321.5 16.5 %multiply_reduce_fusion = (f32[384]{0:T(512)}, bf16[8,24,24,384]{3,2,1,0:T(8,128)(2,1)}, bf16[8,24,24,384]{3,2,1,0:T(8,128)(2,1)S(1)}) fusion(f32[8,24,24,384]{3,2,1,0:T(8,128)} %bitcast.75, f32[384]{0:T(512)} %get-tuple-element.176, f32[8,24,24]{2,1,0:T(8,128)} %and_select_fusion.1, f32[384]{0:T(512)S(1)} %copy-done.62, ...), kind=kOutput, calls=%fused_computation.387 | convolution fusion | flops 5455281664 | bytes 33053184 | tf_op jit(solution)/shard_map/nijh,hc->nijc/dot_general | solution.py:118
  338.0 11.9 %fusion.203 = f32[1536,384]{1,0:T(8,128)} fusion(bf16[8,24,24,384]{3,2,1,0:T(8,128)(2,1)S(1)} %get-tuple-element.205, bf16[8,24,24,1536]{3,2,1,0:T(8,128)(2,1)} %get-tuple-element.208), kind=kOutput, calls=%fused_computation.401 | convolution fusion | flops 5435817984 | bytes 20054016 | tf_op jit(solution)/shard_map/nijh,nijc->hc/dot_general | solution.py:128
  349.9 21.6 %convert_reduce_fusion = (f32[1536]{0:T(1024)}, bf16[8,24,24,1536]{3,2,1,0:T(8,128)(2,1)}) fusion(f32[8,24,24,1536]{3,2,1,0:T(8,128)} %get-tuple-element.209, f32[1536]{0:T(1024)S(1)} %copy-done.85, bf16[8,24,24,384]{3,2,1,0:T(8,128)(2,1)S(1)} %get-tuple-element.205, bf16[1536,384]{1,0:T(8,128)(2,1)S(1)} %copy-done.112), kind=kOutput, calls=%fused_computation.48 | convolution fusion | flops 5527828992 | bytes 47198208 | tf_op jit(solution)/shard_map/nijc,hc->nijh/dot_general | solution.py:129
  371.5 16.5 %fusion.208 = f32[384,1536]{0,1:T(8,128)} fusion(bf16[8,24,24,1536]{3,2,1,0:T(8,128)(2,1)} %get-tuple-element.212, f32[8,24,24,384]{3,2,1,0:T(8,128)} %copy-done.1, f32[384]{0:T(512)S(1)} %copy-done.106, f32[384]{0:T(512)S(1)} %copy-done.64, f32[8,24,24]{2,1,0:T(8,128)S(1)} %copy-done.11, f32[8,24,24]{2,1,0:T(8,128)S(1)} %copy-done.8), kind=kOutput, calls=%fused_computation.402 | convolution fusion | flops 5444665344 | bytes 23632896 | tf_op jit(solution)/shard_map/nijc,nijh->ch/dot_general | solution.py:134
  388.0 15.5 %multiply_reduce_fusion.1 = (f32[384]{0:T(512)}, f32[8,24,24]{2,1,0:T(8,128)S(1)}, f32[8,24,24]{2,1,0:T(8,128)S(1)}, f32[384]{0:T(512)}, f32[8,24,24,384]{3,2,1,0:T(8,128)}) fusion(f32[8,24,24,384]{3,2,1,0:T(8,128)} %copy-done.1, f32[8,24,24]{2,1,0:T(8,128)S(1)} %copy-done.11, f32[8,24,24]{2,1,0:T(8,128)S(1)} %copy-done.8, f32[384]{0:T(512)S(1)} %copy-done.64, ...), kind=kOutput, calls=%fused_computation.389 | convolution fusion | flops 5451732992 | bytes 29569536 | tf_op jit(solution)/shard_map/nijh,ch->nijc/dot_general | solution.py:136
  404.2 36.5 %fusion.105 = (f32[384]{0:T(512)}, f32[384]{0:T(512)}, f32[384]{0:T(512)}, f32[384]{0:T(512)}, f32[384]{0:T(512)}, /*index=5*/f32[384]{0:T(512)}, f32[384]{0:T(5...) fusion(bf16[8,30,24,384]{3,2,1,0:T(8,128)(2,1)} %copy-done, ...), kind=kLoop, calls=%fused_computation.291 | loop fusion | flops 107930880 | bytes 25760256 | tf_op jit(solution)/shard_map/reduce_sum | solution.py:37
  440.7 8.9 %fusion.102 = (f32[384]{0:T(512)}, f32[384]{0:T(512)}, f32[384]{0:T(512)}, f32[384]{0:T(512)}, f32[384]{0:T(512)}, /*index=5*/f32[384]{0:T(512)}, f32[384]{0:T(512)}, f32[384]{0:T(512)}) fusion(f32[8,24,24,384]{3,2,1,0:T(8,128)} %get-tuple-element.200, bf16[8,24,24,384]{3,2,1,0:T(8,128)(2,1)S(1)} %copy-done.3), kind=kLoop, calls=%fused_computation.288 | loop fusion | flops 38925312 | bytes 10629120 | tf_op jit(solution)/shard_map/reduce_sum | solution.py:37
  449.6 8.6 %fusion.40 = (f32[384]{0:T(512)}, f32[384]{0:T(512)}, f32[384]{0:T(512)}, f32[384]{0:T(512)S(1)}, f32[384]{0:T(512)S(1)}, /*index=5*/f32[384]{0:T(512)S(1)}) fusion(f32[8,24,24,384]{3,2,1,0:T(8,128)} %get-tuple-element.200, bf16[8,30,24,384]{3,2,1,0:T(8,128)(2,1)S(1)} %bitcast.71), kind=kLoop, calls=%fused_computation.226 | loop fusion | flops 31848192 | bytes 11510784 | tf_op jit(solution)/shard_map/reduce_sum | solution.py:37
  458.2 33.2 %fusion.84 = (f32[384]{0:T(512)}, f32[384]{0:T(512)}, f32[384]{0:T(512)}, f32[384]{0:T(512)}, f32[384]{0:T(512)}, /*index=5*/f32[384]{0:T(512)}, f32[384]{0:T(51...) fusion(f32[8,24,24,384]{3,2,1,0:T(8,128)} %get-tuple-element.20, ...), kind=kLoop, calls=%fused_computation.270 | loop fusion | flops 95544576 | bytes 11529216 | tf_op jit(solution)/shard_map/reduce_sum | solution.py:37
  491.8 7.1 pad.19
  529.1 9.3 %stack.217 = f32[49,384]{1,0:T(8,128)} concatenate(f32[1,384]{1,0:T(1,128)S(1)} %stack.168, f32[1,384]{1,0:T(1,128)S(1)} %stack.169, f32[1,384]{1,0:T(1,128)} %stack.170, f32[1,384]{1,0:T(1,128)} %stack.171, f32[1,384]{1,0:T(1,128)} %stack.172, f32[1,384]{1,0:T(1,128)} %stack.173, f32[1,384]{1,0:T(1,128)} %stack.174, f32[1,384]{1,0:T(1,128)} %stack.175, f32[1,384]{1,0:T(1,128)} %stack.176, ...), dimensions={0} | concatenate | bytes 150528 | tf_op jit(solution)/shard_map/stack | solution.py:44
  542.6 3.7 all-to-all-start.1
  547.1 184.0 %fusion.195 = bf16[8,24,24,384]{3,2,1,0:T(8,128)(2,1)} fusion(f32[8,24,24,384]{3,2,1,0:T(8,128)} %bitcast.76, f32[8,30,24,384]{3,2,1,0:T(8,128)} %pad.19, f32[8,24,24,384]{3,2,1,0:T(8,128)} %get-tuple-element.200, f32[8,24,24]{2,1,0:T(8,128)} %get-tuple-element.206, f32[384]{0:T(512)} %get-tuple-element.127, f32[384]{0:T(512)} %get-tuple-element.128, ...), kind=kLoop, calls=%fused_computation.381 | loop fusion | flops 176947200 | bytes 69206016 | tf_op jit(solution)/shard_map/convert_element_type | solution.py:150
  731.1 4.5 copy.166
  735.6 4.7 all-to-all-start.3
  740.4 2.6 bitcast_convert_fusion
  747.5 67.7 %all-reduce.5 = (f32[5,384]{1,0:T(8,128)}, f32[1536]{0:T(1024)}) all-reduce(f32[5,384]{1,0:T(8,128)S(1)} %stack.223, f32[1536]{0:T(1024)} %get-tuple-element.211), channel_id=1, replica_groups=mesh['dp'=8,'space'=4] {'dp','space'}, use_global_device_ids=true, to_apply=%region_60.61 | all-reduce | flops 3456 | bytes 27648 | tf_op jit(solution)/shard_map/psum | solution.py:158
  820.7 2.9 multiply_reduce_fusion.6
  824.8 2.9 multiply_reduce_fusion.5
  838.2 4.1 copy.167
  (333 shorter events, 73.6 us)
Async XLA Ops:
  7.2 52.6 %copy-start.60 = (f32[5,12]{1,0:T(8,128)S(1)}, f32[5,12]{1,0:T(8,128)}, u32[]{:S(2)}) copy-start(f32[5,12]{1,0:T(8,128)} %param.26) | copy-start | bytes 724
  7.2 119.4 %copy-start.12 = (f32[49,12]{0,1:T(8,128)S(1)}, f32[49,12]{0,1:T(8,128)}, u32[]{:S(2)}) copy-start(f32[49,12]{0,1:T(8,128)} %param.23) | copy-start | bytes 7060
  7.2 164.1 %copy-start.110 = (f32[48]{0:T(128)S(1)}, f32[48]{0:T(128)}, u32[]{:S(2)}) copy-start(f32[48]{0:T(128)} %param.32) | copy-start | bytes 580
  7.2 44.6 %all-to-all-start = ((bf16[32,6,24,384]{3,2,1,0:T(8,128)(2,1)}), bf16[32,6,24,384]{3,2,1,0:T(8,128)(2,1)S(1)}, u32[]{:S(2)}, u32[]{:S(2)}) async-start(bf16[32,6,24,384]{3,2,1,0:T(8,128)(2,1)} %param.19), calls=%async_computation | async-start | bytes 7077888 | tf_op jit(solution)/shard_map/all_to_all | solution.py:89
  11.6 291.2 %all-gather.5.cloned.1.call-start = ((), (), s32[]{:S(2)}) async-start(), calls=%async_computation.4 | async-start | bytes 1216512 | tf_op jit(solution)/shard_map/all_gather | solution.py:79
  51.9 74.8 %copy-start.4 = (bf16[32,6,24,384]{3,2,1,0:T(8,128)(2,1)}, bf16[32,6,24,384]{3,2,1,0:T(8,128)(2,1)S(1)}, u32[]{:S(2)}) copy-start(bf16[32,6,24,384]{3,2,1,0:T(8,128)(2,1)S(1)} %all-to-all-done) | copy-start | bytes 10616836
  51.9 177.5 %all-to-all-start.2 = ((bf16[32,6,24,384]{3,2,1,0:T(8,128)(2,1)}), bf16[32,6,24,384]{3,2,1,0:T(8,128)(2,1)}, u32[]{:S(2)}, u32[]{:S(2)}) async-start(bf16[32,6,24,384]{3,2,1,0:T(8,128)(2,1)} %param.20), calls=%async_computation.2 | async-start | bytes 7077888 | tf_op jit(solution)/shard_map/all_to_all | solution.py:90
  58.2 263.3 %all-gather.7.cloned.1.call-start = ((), (), s32[]{:S(2)}) async-start(), calls=%async_computation.5 | async-start | bytes 1216512 | tf_op jit(solution)/shard_map/all_gather | solution.py:80
  236.5 61.2 %copy-start = (bf16[8,30,24,384]{3,2,1,0:T(8,128)(2,1)}, bf16[8,30,24,384]{3,2,1,0:T(8,128)(2,1)S(1)}, u32[]{:S(2)}) copy-start(bf16[8,30,24,384]{3,2,1,0:T(8,128)(2,1)S(1)} %pad.17) | copy-start | bytes 13271044
  404.2 36.5 %copy-start.3 = (bf16[8,24,24,384]{3,2,1,0:T(8,128)(2,1)S(1)}, bf16[8,24,24,384]{3,2,1,0:T(8,128)(2,1)}, u32[]{:S(2)}) copy-start(bf16[8,24,24,384]{3,2,1,0:T(8,128)(2,1)} %copy-done.2) | copy-start | bytes 10616836
  491.6 28.2 %copy-start.103 = (f32[384]{0:T(512)S(1)}, f32[384]{0:T(512)}, u32[]{:S(2)}) copy-start(f32[384]{0:T(512)} %get-tuple-element.93) | copy-start | bytes 4612
  491.6 28.2 %copy-start.102 = (f32[384]{0:T(512)S(1)}, f32[384]{0:T(512)}, u32[]{:S(2)}) copy-start(f32[384]{0:T(512)} %get-tuple-element.94) | copy-start | bytes 4612
  491.6 28.8 %copy-start.101 = (f32[384]{0:T(512)S(1)}, f32[384]{0:T(512)}, u32[]{:S(2)}) copy-start(f32[384]{0:T(512)} %get-tuple-element.95) | copy-start | bytes 4612
  491.6 29.4 %copy-start.100 = (f32[384]{0:T(512)S(1)}, f32[384]{0:T(512)}, u32[]{:S(2)}) copy-start(f32[384]{0:T(512)} %get-tuple-element.96) | copy-start | bytes 4612
  491.6 29.9 %copy-start.99 = (f32[384]{0:T(512)S(1)}, f32[384]{0:T(512)}, u32[]{:S(2)}) copy-start(f32[384]{0:T(512)} %get-tuple-element.97) | copy-start | bytes 4612
  491.6 30.5 %copy-start.98 = (f32[384]{0:T(512)S(1)}, f32[384]{0:T(512)}, u32[]{:S(2)}) copy-start(f32[384]{0:T(512)} %get-tuple-element.98) | copy-start | bytes 4612
  491.6 31.1 %copy-start.97 = (f32[384]{0:T(512)S(1)}, f32[384]{0:T(512)}, u32[]{:S(2)}) copy-start(f32[384]{0:T(512)} %get-tuple-element.99) | copy-start | bytes 4612
  491.7 31.7 %copy-start.96 = (f32[384]{0:T(512)S(1)}, f32[384]{0:T(512)}, u32[]{:S(2)}) copy-start(f32[384]{0:T(512)} %get-tuple-element.100) | copy-start | bytes 4612
  491.7 32.3 %copy-start.95 = (f32[384]{0:T(512)S(1)}, f32[384]{0:T(512)}, u32[]{:S(2)}) copy-start(f32[384]{0:T(512)} %get-tuple-element.101) | copy-start | bytes 4612
  491.7 32.9 %copy-start.94 = (f32[384]{0:T(512)S(1)}, f32[384]{0:T(512)}, u32[]{:S(2)}) copy-start(f32[384]{0:T(512)} %get-tuple-element.102) | copy-start | bytes 4612
  491.7 33.4 %copy-start.93 = (f32[384]{0:T(512)S(1)}, f32[384]{0:T(512)}, u32[]{:S(2)}) copy-start(f32[384]{0:T(512)} %get-tuple-element.103) | copy-start | bytes 4612
  491.7 34.0 %copy-start.92 = (f32[384]{0:T(512)S(1)}, f32[384]{0:T(512)}, u32[]{:S(2)}) copy-start(f32[384]{0:T(512)} %get-tuple-element.104) | copy-start | bytes 4612
  491.7 34.5 %copy-start.91 = (f32[384]{0:T(512)S(1)}, f32[384]{0:T(512)}, u32[]{:S(2)}) copy-start(f32[384]{0:T(512)} %get-tuple-element.105) | copy-start | bytes 4612
  491.7 35.1 %copy-start.90 = (f32[384]{0:T(512)S(1)}, f32[384]{0:T(512)}, u32[]{:S(2)}) copy-start(f32[384]{0:T(512)} %get-tuple-element.106) | copy-start | bytes 4612
  491.7 35.7 %copy-start.89 = (f32[384]{0:T(512)S(1)}, f32[384]{0:T(512)}, u32[]{:S(2)}) copy-start(f32[384]{0:T(512)} %get-tuple-element.107) | copy-start | bytes 4612
  491.7 36.2 %copy-start.88 = (f32[384]{0:T(512)S(1)}, f32[384]{0:T(512)}, u32[]{:S(2)}) copy-start(f32[384]{0:T(512)} %get-tuple-element.108) | copy-start | bytes 4612
  491.7 36.8 %copy-start.87 = (f32[384]{0:T(512)S(1)}, f32[384]{0:T(512)}, u32[]{:S(2)}) copy-start(f32[384]{0:T(512)} %get-tuple-element.109) | copy-start | bytes 4612
  491.8 48.4 %copy-start.6 = (bf16[8,24,24,384]{3,2,1,0:T(8,128)(2,1)S(1)}, bf16[8,24,24,384]{3,2,1,0:T(8,128)(2,1)}, u32[]{:S(2)}) copy-start(bf16[8,24,24,384]{3,2,1,0:T(8,128)(2,1)} %get-tuple-element.204) | copy-start | bytes 10616836
  542.6 193.0 %all-to-all-start.1 = ((bf16[8,24,24,384]{3,2,0,1:T(8,128)(2,1)}), bf16[8,24,24,384]{3,2,0,1:T(8,128)(2,1)S(1)}, u32[]{:S(2)}, u32[]{:S(2)}) async-start(bf16[8,24,24,384]{3,2,0,1:T(8,128)(2,1)} %copy.163), calls=%async_computation.1 | async-start | bytes 7077888 | tf_op jit(solution)/shard_map/all_to_all | solution.py:154
  546.3 271.5 %all-reduce.9.cloned.1.call-start = ((), (), s32[]{:S(2)}) async-start(), calls=%async_computation.6 | async-start | bytes 9830400 | tf_op jit(solution)/shard_map/psum | solution.py:158
  735.6 102.6 %all-to-all-start.3 = ((bf16[8,24,24,384]{3,2,0,1:T(8,128)(2,1)}), bf16[8,24,24,384]{3,2,0,1:T(8,128)(2,1)}, u32[]{:S(2)}, u32[]{:S(2)}) async-start(bf16[8,24,24,384]{3,2,0,1:T(8,128)(2,1)} %copy.166), calls=%async_computation.3 | async-start | bytes 7077888 | tf_op jit(solution)/shard_map/all_to_all | solution.py:155
  743.0 86.8 %copy-start.61 = (f32[5,12]{1,0:T(8,128)S(1)}, f32[5,12]{1,0:T(8,128)}, u32[]{:S(2)}) copy-start(f32[5,12]{1,0:T(8,128)} %param.26) | copy-start | bytes 724
  (90 other events, 746.9 us)
Sparse Core Ops, SparseCore 0:
  15.9 54.4 all-gather.4
  73.9 53.8 all-gather.6
  553.3 147.8 all-reduce.8
where the time goes:
time: 862 us; the launch traced here: 850 us
  other arithmetic  362 us (42%)
  blocking collectives  221 us (26%)
  matrix products  101 us (12%)
  local copies, waits for them, and re-layouts  88.7 us (10%)
  waiting for transfers between devices  39.5 us (5%)
  between operations  19.9 us (2%)
  starting transfers between devices  19.2 us (2%)
    convert_element_type x1, other arithmetic, body(): (grad_out + pixel_mask[..., None] * grad_u).astype(jnp.bfloat16)  184 us
    reduce_sum x4, other arithmetic, kernel_grad(): jnp.sum(wide[:, row_off:row_off + out_rows, col_off:col_off + out_cols, :...  87.2 us
    psum x1, blocking collectives, body(): lax.psum((local_grads[0], local_grads[1], local_grads[2], local_grads[3],...  67.7 us
    all_gather x1, blocking collectives, body(): lax.all_gather(block_vectors, ('dp', 'space'), axis=1, tiled=True)  64.6 us
    reduce_sum x1, other arithmetic, body(): chan_mean = jnp.mean(conv, axis=-1, keepdims=True)  59.4 us
    unnamed x1, blocking collectives  45.5 us
    all_gather x1, blocking collectives, body(): lax.all_gather(depth_kernel, ('dp', 'space'), axis=1, tiled=True)  43 us
    another operation x51, local copies, waits for them, and re-layouts, kernel_grad(): return jnp.stack(pieces)  41.1 us
  transfers between devices with their start and end apart: 7, of which 1 were waited for; matrix products, arithmetic and copies ran while one was open for 38% of the time, Pallas kernels for 0%

commit v1 on v0

--- a/solution.py
+++ b/solution.py
@@ -14,6 +14,14 @@
 step_rates = (0.15, 0.5, 0.05, 0.2, 0.025)
 inv_root_two = 0.7071067811865476
 inv_root_tau = 0.3989422804014327
+
+
+def rest_the_local_data(point, bus_axis):
+    prior = jnp.concatenate(
+        lax.all_to_all(jnp.stack(jnp.split(point, lax.psum(1, bus_axis), axis=0)), bus_axis, 0, 0),
+        axis=1,
+    )
+    return prior
 
 
 def conv_rows(padded, kernel, out_rows, out_cols):
@@ -86,7 +94,7 @@
     )
     map_side = images.shape[2]
     local_images, local_cot = (
-        lax.all_to_all(images, "space", split_axis=0, concat_axis=1, tiled=True),
+        rest_the_local_data(images, "space"),
         lax.all_to_all(cotangent, "space", split_axis=0, concat_axis=1, tiled=True),
     )
     img_count = local_images.shape[0]

time: 862 us -> 859 us (level)
  no operation moved by 1% of the time
where the time goes in v1:
time: 859 us; the launch traced here: 855 us
  other arithmetic  364 us (42%)
  blocking collectives  221 us (26%)
  matrix products  101 us (12%)
  local copies, waits for them, and re-layouts  91 us (11%)
  waiting for transfers between devices  39.5 us (5%)
  between operations  19.7 us (2%)
  starting transfers between devices  19.2 us (2%)
    convert_element_type x1, other arithmetic, body(): (grad_out + pixel_mask[..., None] * grad_u).astype(jnp.bfloat16)  184 us
    reduce_sum x4, other arithmetic, kernel_grad(): jnp.sum(wide[:, row_off:row_off + out_rows, col_off:col_off + out_cols, :...  87.2 us
    psum x1, blocking collectives, body(): lax.psum((local_grads[0], local_grads[1], local_grads[2], local_grads[3],...  67.7 us
    all_gather x1, blocking collectives, body(): lax.all_gather(block_vectors, ('dp', 'space'), axis=1, tiled=True)  64.6 us
    reduce_sum x1, other arithmetic, body(): chan_mean = jnp.mean(conv, axis=-1, keepdims=True)  59.4 us
    unnamed x1, blocking collectives  45.7 us
    all_gather x1, blocking collectives, body(): lax.all_gather(depth_kernel, ('dp', 'space'), axis=1, tiled=True)  43 us
    another operation x51, local copies, waits for them, and re-layouts, kernel_grad(): return jnp.stack(pieces)  41.1 us
  transfers between devices with their start and end apart: 7, of which 1 were waited for; matrix products, arithmetic and copies ran while one was open for 38% of the time, Pallas kernels for 0%

profile of v1, /device:TPU:12, one launch (start us, length us, event | category | flops | bytes accessed | tf_op | source)
XLA Modules:
  0.0 854.7 jit_solution(6520246456851592320)
XLA Ops:
  11.6 4.3 all-to-all-start
  17.5 38.7 %all-to-all-done = bf16[4,8,6,24,384]{4,3,2,1,0:T(8,128)(2,1)S(1)} async-done(((bf16[4,8,6,24,384]{4,3,2,1,0:T(8,128)(2,1)}), bf16[4,8,6,24,384]{4,3,2,1,0:T(8,128)(2,1)S(1)}, u32[]{:S(2)}, u32[]{:S(2)}) %all-to-all-start) | async-done | bytes 3538976 | tf_op jit(solution)/shard_map/all_to_all | solution.py:21
  56.2 6.4 all-to-all-start.2
  64.2 64.6 %all-gather = f32[32,12,5]{1,2,0:T(8,128)S(1)} all-gather(f32[1,12,5]{1,2,0:T(8,128)S(1)} %bitcast.89), channel_id=1, replica_groups=mesh['dp'=8,'space'=4] {'dp','space'}, dimensions={0}, use_global_device_ids=true | all-gather | bytes 7920 | tf_op jit(solution)/shard_map/all_gather | solution.py:92
  131.0 43.0 %all-gather.1 = f32[32,12,49]{2,1,0:T(8,128)} all-gather(f32[1,12,49]{2,1,0:T(8,128)S(1)} %bitcast.87), channel_id=1, replica_groups=mesh['dp'=8,'space'=4] {'dp','space'}, dimensions={0}, use_global_device_ids=true | all-gather | bytes 77616 | tf_op jit(solution)/shard_map/all_gather | solution.py:91
  175.9 45.7 %all-reduce.4 = f32[1536]{0:T(1024)} all-reduce(f32[1536]{0:T(1024)S(1)} %dynamic-update-slice), channel_id=1, replica_groups=mesh['dp'=8,'space'=4] {'dp','space'}, use_global_device_ids=true, to_apply=%add.4 | all-reduce | flops 1536 | bytes 12288
  225.9 2.6 slice_reduce_fusion.47
  228.5 2.6 slice_reduce_fusion.48
  233.9 5.5 copy.165
  242.8 59.4 %fusion.231 = (f32[8,24,24]{2,1,0:T(8,128)S(1)}, f32[8,24,24,384]{3,2,1,0:T(8,128)S(1)}) fusion(f32[384]{0:T(512)} %get-tuple-element.179, f32[384]{0:T(512)S(1)} %copy-done.48, f32[384]{0:T(512)S(1)} %copy-done.49, f32[384]{0:T(512)S(1)} %copy-done.50, bf16[8,30,24,384]{3,2,1,0:T(8,128)(2,1)S(1)} %pad.17, f32[384]{0:T(512)S(1)} %copy-done.51, ...), kind=kLoop, calls=%fused_computation.512 | loop fusion | flops 267185664 | bytes 36440576 | tf_op jit(solution)/shard_map/reduce_sum | solution.py:114
  302.3 2.8 copy-done.1
  307.4 18.7 %multiply_convert_fusion = (bf16[8,24,24,1536]{3,2,1,0:T(8,128)(2,1)}, f32[8,24,24,1536]{3,2,1,0:T(8,128)}) fusion(f32[1536]{0:T(1024)S(1)} %copy-done.85, bf16[384,1536]{0,1:T(8,128)(2,1)} %all-gather.5.cloned.1.call-done, f32[8,24,24,384]{3,2,1,0:T(8,128)} %copy-done.1, f32[384]{0:T(512)} %get-tuple-element.177, f32[384]{0:T(512)S(1)} %copy-done.64, ...), kind=kOutput, calls=%fused_computation.49 | convolution fusion | flops 5487132672 | bytes 50770944 | tf_op jit(solution)/shard_map/nijc,ch->nijh/dot_general | solution.py:121
  326.0 16.5 %multiply_reduce_fusion = (f32[384]{0:T(512)}, bf16[8,24,24,384]{3,2,1,0:T(8,128)(2,1)}, bf16[8,24,24,384]{3,2,1,0:T(8,128)(2,1)S(1)}) fusion(f32[8,24,24,384]{3,2,1,0:T(8,128)} %bitcast.81, f32[384]{0:T(512)} %get-tuple-element.176, f32[8,24,24]{2,1,0:T(8,128)} %and_select_fusion.1, f32[384]{0:T(512)S(1)} %copy-done.62, ...), kind=kOutput, calls=%fused_computation.387 | convolution fusion | flops 5455281664 | bytes 33053184 | tf_op jit(solution)/shard_map/nijh,hc->nijc/dot_general | solution.py:126
  342.5 11.9 %fusion.203 = f32[1536,384]{1,0:T(8,128)} fusion(bf16[8,24,24,384]{3,2,1,0:T(8,128)(2,1)S(1)} %get-tuple-element.205, bf16[8,24,24,1536]{3,2,1,0:T(8,128)(2,1)} %get-tuple-element.212), kind=kOutput, calls=%fused_computation.402 | convolution fusion | flops 5435817984 | bytes 20054016 | tf_op jit(solution)/shard_map/nijh,nijc->hc/dot_general | solution.py:136
  354.4 21.6 %convert_reduce_fusion = (f32[1536]{0:T(1024)}, bf16[8,24,24,1536]{3,2,1,0:T(8,128)(2,1)}) fusion(f32[8,24,24,1536]{3,2,1,0:T(8,128)} %get-tuple-element.213, f32[1536]{0:T(1024)S(1)} %copy-done.85, bf16[8,24,24,384]{3,2,1,0:T(8,128)(2,1)S(1)} %get-tuple-element.205, bf16[1536,384]{1,0:T(8,128)(2,1)S(1)} %copy-done.112), kind=kOutput, calls=%fused_computation.48 | convolution fusion | flops 5527828992 | bytes 47198208 | tf_op jit(solution)/shard_map/nijc,hc->nijh/dot_general | solution.py:137
  376.0 16.5 %fusion.208 = f32[384,1536]{0,1:T(8,128)} fusion(bf16[8,24,24,1536]{3,2,1,0:T(8,128)(2,1)} %get-tuple-element.216, f32[8,24,24,384]{3,2,1,0:T(8,128)} %copy-done.1, f32[384]{0:T(512)S(1)} %copy-done.106, f32[384]{0:T(512)S(1)} %copy-done.64, f32[8,24,24]{2,1,0:T(8,128)S(1)} %copy-done.11, f32[8,24,24]{2,1,0:T(8,128)S(1)} %copy-done.8), kind=kOutput, calls=%fused_computation.403 | convolution fusion | flops 5444665344 | bytes 23632896 | tf_op jit(solution)/shard_map/nijc,nijh->ch/dot_general | solution.py:142
  392.5 15.5 %multiply_reduce_fusion.1 = (f32[384]{0:T(512)}, f32[8,24,24]{2,1,0:T(8,128)S(1)}, f32[8,24,24]{2,1,0:T(8,128)S(1)}, f32[384]{0:T(512)}, f32[8,24,24,384]{3,2,1,0:T(8,128)}) fusion(f32[8,24,24,384]{3,2,1,0:T(8,128)} %copy-done.1, f32[8,24,24]{2,1,0:T(8,128)S(1)} %copy-done.11, f32[8,24,24]{2,1,0:T(8,128)S(1)} %copy-done.8, f32[384]{0:T(512)S(1)} %copy-done.64, ...), kind=kOutput, calls=%fused_computation.389 | convolution fusion | flops 5451732992 | bytes 29569536 | tf_op jit(solution)/shard_map/nijh,ch->nijc/dot_general | solution.py:144
  408.8 36.5 %fusion.105 = (f32[384]{0:T(512)}, f32[384]{0:T(512)}, f32[384]{0:T(512)}, f32[384]{0:T(512)}, f32[384]{0:T(512)}, /*index=5*/f32[384]{0:T(512)}, f32[384]{0:T(5...) fusion(bf16[8,30,24,384]{3,2,1,0:T(8,128)(2,1)} %copy-done, ...), kind=kLoop, calls=%fused_computation.291 | loop fusion | flops 107930880 | bytes 25760256 | tf_op jit(solution)/shard_map/reduce_sum | solution.py:45
  445.2 8.9 %fusion.102 = (f32[384]{0:T(512)}, f32[384]{0:T(512)}, f32[384]{0:T(512)}, f32[384]{0:T(512)}, f32[384]{0:T(512)}, /*index=5*/f32[384]{0:T(512)}, f32[384]{0:T(512)}, f32[384]{0:T(512)}) fusion(f32[8,24,24,384]{3,2,1,0:T(8,128)} %get-tuple-element.200, bf16[8,24,24,384]{3,2,1,0:T(8,128)(2,1)S(1)} %copy-done.3), kind=kLoop, calls=%fused_computation.288 | loop fusion | flops 38925312 | bytes 10629120 | tf_op jit(solution)/shard_map/reduce_sum | solution.py:45
  454.1 8.6 %fusion.40 = (f32[384]{0:T(512)}, f32[384]{0:T(512)}, f32[384]{0:T(512)}, f32[384]{0:T(512)S(1)}, f32[384]{0:T(512)S(1)}, /*index=5*/f32[384]{0:T(512)S(1)}) fusion(f32[8,24,24,384]{3,2,1,0:T(8,128)} %get-tuple-element.200, bf16[8,30,24,384]{3,2,1,0:T(8,128)(2,1)S(1)} %bitcast.77), kind=kLoop, calls=%fused_computation.226 | loop fusion | flops 31848192 | bytes 11510784 | tf_op jit(solution)/shard_map/reduce_sum | solution.py:45
  462.8 33.2 %fusion.84 = (f32[384]{0:T(512)}, f32[384]{0:T(512)}, f32[384]{0:T(512)}, f32[384]{0:T(512)}, f32[384]{0:T(512)}, /*index=5*/f32[384]{0:T(512)}, f32[384]{0:T(51...) fusion(f32[8,24,24,384]{3,2,1,0:T(8,128)} %get-tuple-element.20, ...), kind=kLoop, calls=%fused_computation.270 | loop fusion | flops 95544576 | bytes 11529216 | tf_op jit(solution)/shard_map/reduce_sum | solution.py:45
  496.3 7.1 pad.19
  533.7 9.3 %stack.237 = f32[49,384]{1,0:T(8,128)} concatenate(f32[1,384]{1,0:T(1,128)S(1)} %stack.188, f32[1,384]{1,0:T(1,128)S(1)} %stack.189, f32[1,384]{1,0:T(1,128)} %stack.190, f32[1,384]{1,0:T(1,128)} %stack.191, f32[1,384]{1,0:T(1,128)} %stack.192, f32[1,384]{1,0:T(1,128)} %stack.193, f32[1,384]{1,0:T(1,128)} %stack.194, f32[1,384]{1,0:T(1,128)} %stack.195, f32[1,384]{1,0:T(1,128)} %stack.196, ...), dimensions={0} | concatenate | bytes 150528 | tf_op jit(solution)/shard_map/stack | solution.py:52
  547.1 3.7 all-to-all-start.1
  551.6 184.0 %fusion.195 = bf16[8,24,24,384]{3,2,1,0:T(8,128)(2,1)} fusion(f32[8,24,24,384]{3,2,1,0:T(8,128)} %bitcast.82, f32[8,30,24,384]{3,2,1,0:T(8,128)} %pad.19, f32[8,24,24,384]{3,2,1,0:T(8,128)} %get-tuple-element.200, f32[8,24,24]{2,1,0:T(8,128)} %get-tuple-element.210, f32[384]{0:T(512)} %get-tuple-element.127, f32[384]{0:T(512)} %get-tuple-element.128, ...), kind=kLoop, calls=%fused_computation.381 | loop fusion | flops 176947200 | bytes 69206016 | tf_op jit(solution)/shard_map/convert_element_type | solution.py:158
  735.7 4.5 copy.166
  740.1 4.7 all-to-all-start.3
  744.9 2.6 bitcast_convert_fusion
  752.0 67.7 %all-reduce.5 = (f32[5,384]{1,0:T(8,128)}, f32[1536]{0:T(1024)}) all-reduce(f32[5,384]{1,0:T(8,128)S(1)} %stack.243, f32[1536]{0:T(1024)} %get-tuple-element.215), channel_id=1, replica_groups=mesh['dp'=8,'space'=4] {'dp','space'}, use_global_device_ids=true, to_apply=%region_60.61 | all-reduce | flops 3456 | bytes 27648 | tf_op jit(solution)/shard_map/psum | solution.py:166
  825.2 2.9 multiply_reduce_fusion.6
  829.4 2.9 multiply_reduce_fusion.5
  842.7 4.1 copy.167
  (335 shorter events, 78.0 us)
Async XLA Ops:
  11.6 52.5 %copy-start.60 = (f32[5,12]{1,0:T(8,128)S(1)}, f32[5,12]{1,0:T(8,128)}, u32[]{:S(2)}) copy-start(f32[5,12]{1,0:T(8,128)} %param.26) | copy-start | bytes 724
  11.6 119.4 %copy-start.12 = (f32[49,12]{0,1:T(8,128)S(1)}, f32[49,12]{0,1:T(8,128)}, u32[]{:S(2)}) copy-start(f32[49,12]{0,1:T(8,128)} %param.23) | copy-start | bytes 7060
  11.6 164.1 %copy-start.110 = (f32[48]{0:T(128)S(1)}, f32[48]{0:T(128)}, u32[]{:S(2)}) copy-start(f32[48]{0:T(128)} %param.32) | copy-start | bytes 580
  11.6 44.6 %all-to-all-start = ((bf16[4,8,6,24,384]{4,3,2,1,0:T(8,128)(2,1)}), bf16[4,8,6,24,384]{4,3,2,1,0:T(8,128)(2,1)S(1)}, u32[]{:S(2)}, u32[]{:S(2)}) async-start(bf16[4,8,6,24,384]{4,3,2,1,0:T(8,128)(2,1)} %pad_maximum_fusion), calls=%async_computation | async-start | bytes 7077888 | tf_op jit(solution)/shard_map/all_to_all | solution.py:21
  16.0 291.4 %all-gather.5.cloned.1.call-start = ((), (), s32[]{:S(2)}) async-start(), calls=%async_computation.4 | async-start | bytes 1216512 | tf_op jit(solution)/shard_map/all_gather | solution.py:87
  56.2 74.8 %copy-start.4 = (bf16[4,8,6,24,384]{4,3,2,1,0:T(8,128)(2,1)}, bf16[4,8,6,24,384]{4,3,2,1,0:T(8,128)(2,1)S(1)}, u32[]{:S(2)}) copy-start(bf16[4,8,6,24,384]{4,3,2,1,0:T(8,128)(2,1)S(1)} %all-to-all-done) | copy-start | bytes 10616836
  56.2 177.7 %all-to-all-start.2 = ((bf16[32,6,24,384]{3,2,1,0:T(8,128)(2,1)}), bf16[32,6,24,384]{3,2,1,0:T(8,128)(2,1)}, u32[]{:S(2)}, u32[]{:S(2)}) async-start(bf16[32,6,24,384]{3,2,1,0:T(8,128)(2,1)} %param.20), calls=%async_computation.2 | async-start | bytes 7077888 | tf_op jit(solution)/shard_map/all_to_all | solution.py:98
  62.6 263.4 %all-gather.7.cloned.1.call-start = ((), (), s32[]{:S(2)}) async-start(), calls=%async_computation.5 | async-start | bytes 1216512 | tf_op jit(solution)/shard_map/all_gather | solution.py:88
  241.0 61.2 %copy-start = (bf16[8,30,24,384]{3,2,1,0:T(8,128)(2,1)}, bf16[8,30,24,384]{3,2,1,0:T(8,128)(2,1)S(1)}, u32[]{:S(2)}) copy-start(bf16[8,30,24,384]{3,2,1,0:T(8,128)(2,1)S(1)} %pad.17) | copy-start | bytes 13271044
  408.8 36.5 %copy-start.3 = (bf16[8,24,24,384]{3,2,1,0:T(8,128)(2,1)S(1)}, bf16[8,24,24,384]{3,2,1,0:T(8,128)(2,1)}, u32[]{:S(2)}) copy-start(bf16[8,24,24,384]{3,2,1,0:T(8,128)(2,1)} %copy-done.2) | copy-start | bytes 10616836
  496.1 28.2 %copy-start.103 = (f32[384]{0:T(512)S(1)}, f32[384]{0:T(512)}, u32[]{:S(2)}) copy-start(f32[384]{0:T(512)} %get-tuple-element.93) | copy-start | bytes 4612
  496.1 28.2 %copy-start.102 = (f32[384]{0:T(512)S(1)}, f32[384]{0:T(512)}, u32[]{:S(2)}) copy-start(f32[384]{0:T(512)} %get-tuple-element.94) | copy-start | bytes 4612
  496.1 28.8 %copy-start.101 = (f32[384]{0:T(512)S(1)}, f32[384]{0:T(512)}, u32[]{:S(2)}) copy-start(f32[384]{0:T(512)} %get-tuple-element.95) | copy-start | bytes 4612
  496.2 29.4 %copy-start.100 = (f32[384]{0:T(512)S(1)}, f32[384]{0:T(512)}, u32[]{:S(2)}) copy-start(f32[384]{0:T(512)} %get-tuple-element.96) | copy-start | bytes 4612
  496.2 29.9 %copy-start.99 = (f32[384]{0:T(512)S(1)}, f32[384]{0:T(512)}, u32[]{:S(2)}) copy-start(f32[384]{0:T(512)} %get-tuple-element.97) | copy-start | bytes 4612
  496.2 30.5 %copy-start.98 = (f32[384]{0:T(512)S(1)}, f32[384]{0:T(512)}, u32[]{:S(2)}) copy-start(f32[384]{0:T(512)} %get-tuple-element.98) | copy-start | bytes 4612
  496.2 31.1 %copy-start.97 = (f32[384]{0:T(512)S(1)}, f32[384]{0:T(512)}, u32[]{:S(2)}) copy-start(f32[384]{0:T(512)} %get-tuple-element.99) | copy-start | bytes 4612
  496.2 31.7 %copy-start.96 = (f32[384]{0:T(512)S(1)}, f32[384]{0:T(512)}, u32[]{:S(2)}) copy-start(f32[384]{0:T(512)} %get-tuple-element.100) | copy-start | bytes 4612
  496.2 32.3 %copy-start.95 = (f32[384]{0:T(512)S(1)}, f32[384]{0:T(512)}, u32[]{:S(2)}) copy-start(f32[384]{0:T(512)} %get-tuple-element.101) | copy-start | bytes 4612
  496.2 32.9 %copy-start.94 = (f32[384]{0:T(512)S(1)}, f32[384]{0:T(512)}, u32[]{:S(2)}) copy-start(f32[384]{0:T(512)} %get-tuple-element.102) | copy-start | bytes 4612
  496.2 33.4 %copy-start.93 = (f32[384]{0:T(512)S(1)}, f32[384]{0:T(512)}, u32[]{:S(2)}) copy-start(f32[384]{0:T(512)} %get-tuple-element.103) | copy-start | bytes 4612
  496.2 34.0 %copy-start.92 = (f32[384]{0:T(512)S(1)}, f32[384]{0:T(512)}, u32[]{:S(2)}) copy-start(f32[384]{0:T(512)} %get-tuple-element.104) | copy-start | bytes 4612
  496.2 34.5 %copy-start.91 = (f32[384]{0:T(512)S(1)}, f32[384]{0:T(512)}, u32[]{:S(2)}) copy-start(f32[384]{0:T(512)} %get-tuple-element.105) | copy-start | bytes 4612
  496.3 35.1 %copy-start.90 = (f32[384]{0:T(512)S(1)}, f32[384]{0:T(512)}, u32[]{:S(2)}) copy-start(f32[384]{0:T(512)} %get-tuple-element.106) | copy-start | bytes 4612
  496.3 35.7 %copy-start.89 = (f32[384]{0:T(512)S(1)}, f32[384]{0:T(512)}, u32[]{:S(2)}) copy-start(f32[384]{0:T(512)} %get-tuple-element.107) | copy-start | bytes 4612
  496.3 36.2 %copy-start.88 = (f32[384]{0:T(512)S(1)}, f32[384]{0:T(512)}, u32[]{:S(2)}) copy-start(f32[384]{0:T(512)} %get-tuple-element.108) | copy-start | bytes 4612
  496.3 36.8 %copy-start.87 = (f32[384]{0:T(512)S(1)}, f32[384]{0:T(512)}, u32[]{:S(2)}) copy-start(f32[384]{0:T(512)} %get-tuple-element.109) | copy-start | bytes 4612
  496.3 48.4 %copy-start.6 = (bf16[8,24,24,384]{3,2,1,0:T(8,128)(2,1)S(1)}, bf16[8,24,24,384]{3,2,1,0:T(8,128)(2,1)}, u32[]{:S(2)}) copy-start(bf16[8,24,24,384]{3,2,1,0:T(8,128)(2,1)} %get-tuple-element.204) | copy-start | bytes 10616836
  547.1 193.0 %all-to-all-start.1 = ((bf16[8,24,24,384]{3,2,0,1:T(8,128)(2,1)}), bf16[8,24,24,384]{3,2,0,1:T(8,128)(2,1)S(1)}, u32[]{:S(2)}, u32[]{:S(2)}) async-start(bf16[8,24,24,384]{3,2,0,1:T(8,128)(2,1)} %copy.163), calls=%async_computation.1 | async-start | bytes 7077888 | tf_op jit(solution)/shard_map/all_to_all | solution.py:162
  550.9 271.5 %all-reduce.9.cloned.1.call-start = ((), (), s32[]{:S(2)}) async-start(), calls=%async_computation.6 | async-start | bytes 9830400 | tf_op jit(solution)/shard_map/psum | solution.py:166
  740.1 102.6 %all-to-all-start.3 = ((bf16[8,24,24,384]{3,2,0,1:T(8,128)(2,1)}), bf16[8,24,24,384]{3,2,0,1:T(8,128)(2,1)}, u32[]{:S(2)}, u32[]{:S(2)}) async-start(bf16[8,24,24,384]{3,2,0,1:T(8,128)(2,1)} %copy.166), calls=%async_computation.3 | async-start | bytes 7077888 | tf_op jit(solution)/shard_map/all_to_all | solution.py:163
  747.6 86.8 %copy-start.61 = (f32[5,12]{1,0:T(8,128)S(1)}, f32[5,12]{1,0:T(8,128)}, u32[]{:S(2)}) copy-start(f32[5,12]{1,0:T(8,128)} %param.26) | copy-start | bytes 724
  (90 other events, 746.9 us)
Sparse Core Ops, SparseCore 0:
  20.3 54.4 all-gather.4
  78.3 53.8 all-gather.6
  557.8 147.8 all-reduce.8
